TPU v7x, 512 devices: a whole 4x4x16 slice. The times are simulated.
512 devices in a mesh: dp: 32 (over z, core), seq: 16 (over y, x).
Axes of the slice: x: 4, y: 4, z: 16, core: 2. Of those that a mesh axis runs over, the one named last changes fastest.
Arguments:
- q_pre: bfloat16 [32, 2048, 16, 128], P('dp', 'seq'), may hold values from -6 to 6
- k_pre: bfloat16 [32, 2048, 8, 128], P('dp', 'seq'), may hold values from -6 to 6
- values: bfloat16 [32, 2048, 8, 128], P('dp', 'seq'), may hold values from -6 to 6
- grad_out: bfloat16 [32, 2048, 16, 128], P('dp', 'seq'), may hold values from -6 to 6
- segment_ids: int32 [32, 2048], P('dp', 'seq'), may hold values from 0 to 7, never falling along the last dimension, each value on 1 to 1024 neighbouring positions
- q_gain: float32 [128], replicated, may hold values from 0.1 to 1.9
- k_gain: float32 [128], replicated, may hold values from 0.1 to 1.9
Outputs:
- grad_q: bfloat16 [32, 2048, 16, 128], P('dp', 'seq')
- grad_k: bfloat16 [32, 2048, 8, 128], P('dp', 'seq')
- grad_v: bfloat16 [32, 2048, 8, 128], P('dp', 'seq')
- grad_q_gain: float32 [128], replicated
- grad_k_gain: float32 [128], replicated
Inputs may be any that keep to these rules, and one draw needn't show every extreme that they name: `segment_ids`: along a span the ids never fall, and each id from 0 to 7 names one run of consecutive tokens.
All inputs are finite; a program needn't handle non-finite values.
Results may differ from a plain program's by a relative error of at most 0.017.
Values may be sent and summed in bfloat16 or wider, within the bound.
A program may use at most 64 MiB of HBM per device.

v0:
```python
import jax
import jax.numpy as jnp
from jax import lax
from jax.sharding import PartitionSpec as P

PRESCALE = 168
DOCS = 8
norm_epsilon = 1e-06
rope_base = 1000000.0
rope_factor = 8.0


def document_positions(segments, docs):
    labels = jnp.arange(docs, dtype=jnp.int32)
    member = (segments[:, None] == labels[None, :]).astype(jnp.int32)
    counts = jnp.sum(member, axis=0)
    starts = jnp.cumsum(counts) - counts
    first = jnp.sum(member * starts[None, :], axis=1)
    return (jnp.arange(segments.shape[0], dtype=jnp.int32) - first, first)


def embed(rows, gain, positions):
    width = rows.shape[-1]
    half = width // 2
    scale = lax.rsqrt(jnp.mean(rows * rows, axis=-1, keepdims=True) + norm_epsilon)
    normed = rows * scale * gain
    freqs = rope_base ** (-(jnp.arange(half, dtype=jnp.float32) * 2.0 / width))
    angles = (positions.astype(jnp.float32) / rope_factor)[:, None] * freqs[None, :]
    cosine = jnp.cos(angles)[:, None, :]
    sine = jnp.sin(angles)[:, None, :]
    first_half = normed[..., :half]
    second_half = normed[..., half:]
    return jnp.concatenate(
        [first_half * cosine - second_half * sine, second_half * cosine + first_half * sine],
        axis=-1,
    )


def attend_blocks(queries, keys, vals, upstream, segments):
    total = queries.shape[0]
    group = queries.shape[1]
    width = queries.shape[2]
    block = min(512, total)
    count = total // block
    rows = block * group
    score_scale = float(PRESCALE) ** (-0.5)
    contract_last = (((1,), (1,)), ((), ()))
    contract_first = (((0,), (0,)), ((), ()))

    def query_block(query_index, carry):
        query_grads, key_grads, value_grads = carry
        start = query_index * block
        query_rows = lax.dynamic_slice_in_dim(queries, start, block, 0).reshape(rows, width)
        upstream_rows = lax.dynamic_slice_in_dim(upstream, start, block, 0).reshape(rows, width)
        query_segs = jnp.repeat(lax.dynamic_slice_in_dim(segments, start, block, 0), group)
        query_places = jnp.repeat(start + jnp.arange(block, dtype=jnp.int32), group)
        lower = 0

        def key_scores(key_index):
            key_start = key_index * block
            key_rows = lax.dynamic_slice_in_dim(keys, key_start, block, 0)
            value_rows = lax.dynamic_slice_in_dim(vals, key_start, block, 0)
            key_segs = lax.dynamic_slice_in_dim(segments, key_start, block, 0)
            key_places = key_start + jnp.arange(block, dtype=jnp.int32)
            scores = score_scale * lax.dot_general(
                query_rows, key_rows, contract_last, preferred_element_type=jnp.float32
            )
            visible = (query_segs[:, None] == key_segs[None, :]) & (
                query_places[:, None] >= key_places[None, :]
            )
            return (scores, visible, key_rows, value_rows, key_start)

        def forward_step(key_index, state):
            totals, numer = state
            scores, visible, key_rows, value_rows, key_start = key_scores(key_index)
            raw = jnp.where(visible, jnp.exp(scores), 0.0)
            numer = numer + jnp.dot(
                raw.astype(jnp.bfloat16), value_rows, preferred_element_type=jnp.float32
            )
            return (totals + jnp.sum(raw, axis=1), numer)

        totals, numer = lax.fori_loop(
            lower,
            query_index + 1,
            forward_step,
            (jnp.zeros((rows,), jnp.float32), jnp.zeros((rows, width), jnp.float32)),
        )
        outputs = numer / totals[:, None]
        delta = jnp.sum(upstream_rows.astype(jnp.float32) * outputs, axis=1)
        logsum = jnp.log(totals)

        def backward_step(key_index, state):
            query_part, key_acc, value_acc = state
            scores, visible, key_rows, value_rows, key_start = key_scores(key_index)
            probs = jnp.where(visible, jnp.exp(scores - logsum[:, None]), 0.0).astype(jnp.bfloat16)
            prob_grads = lax.dot_general(
                upstream_rows, value_rows, contract_last, preferred_element_type=jnp.float32
            )
            score_grads = (
                probs.astype(jnp.float32) * (prob_grads - delta[:, None]) * score_scale
            ).astype(jnp.bfloat16)
            query_part = query_part + jnp.dot(
                score_grads, key_rows, preferred_element_type=jnp.float32
            )
            key_part = lax.dot_general(
                score_grads, query_rows, contract_first, preferred_element_type=jnp.float32
            )
            value_part = lax.dot_general(
                probs, upstream_rows, contract_first, preferred_element_type=jnp.float32
            )
            key_acc = lax.dynamic_update_slice_in_dim(
                key_acc,
                lax.dynamic_slice_in_dim(key_acc, key_start, block, 0) + key_part,
                key_start,
                0,
            )
            value_acc = lax.dynamic_update_slice_in_dim(
                value_acc,
                lax.dynamic_slice_in_dim(value_acc, key_start, block, 0) + value_part,
                key_start,
                0,
            )
            return (query_part, key_acc, value_acc)

        query_part, key_grads, value_grads = lax.fori_loop(
            lower,
            query_index + 1,
            backward_step,
            (jnp.zeros((rows, width), jnp.float32), key_grads, value_grads),
        )
        query_grads = lax.dynamic_update_slice_in_dim(query_grads, query_part, start * group, 0)
        return (query_grads, key_grads, value_grads)

    initial = (
        jnp.zeros((total * group, width), jnp.float32),
        jnp.zeros((total, width), jnp.float32),
        jnp.zeros((total, width), jnp.float32),
    )
    query_grads, key_grads, value_grads = lax.fori_loop(0, count, query_block, initial)
    return (query_grads.reshape(total, group, width), key_grads, value_grads)


def body(q_pre, k_pre, values, grad_out, segment_ids, q_gain, k_gain):
    segments = lax.all_gather(segment_ids, "seq", axis=1, tiled=True)[0]
    positions, first = document_positions(segments, DOCS)
    local = q_pre.shape[1]
    heads = q_pre.shape[2]
    kv_heads = k_pre.shape[2]
    width = q_pre.shape[3]
    group = heads // kv_heads

    def embed_rows(rows, gain):
        return embed(rows, gain, positions)

    key_copies = jnp.repeat(k_pre[0], group, axis=1)
    value_copies = jnp.repeat(values[0], group, axis=1)
    query_here, upstream_here, key_here, value_here = (
        lax.all_to_all(q_pre[0], "seq", split_axis=1, concat_axis=0, tiled=True),
        lax.all_to_all(grad_out[0], "seq", split_axis=1, concat_axis=0, tiled=True),
        lax.all_to_all(key_copies, "seq", split_axis=1, concat_axis=0, tiled=True),
        lax.all_to_all(value_copies, "seq", split_axis=1, concat_axis=0, tiled=True),
    )
    query_rot, query_back = jax.vjp(embed_rows, query_here.astype(jnp.float32), q_gain)
    key_rot, key_back = jax.vjp(embed_rows, key_here.astype(jnp.float32), k_gain)
    query_hat = query_rot.astype(jnp.bfloat16)
    key_hat = key_rot.astype(jnp.bfloat16)
    query_list, key_list, value_list = ([], [], [])
    query_part, key_part, value_part = attend_blocks(
        query_hat, key_hat[:, 0], value_here[:, 0], upstream_here, segments
    )
    query_list.append(query_part)
    key_list.append(key_part)
    value_list.append(value_part)
    query_input, query_gain_part = query_back(query_list[0])
    key_input, key_gain_part = key_back(jnp.stack(key_list, axis=1))
    value_input = jnp.stack(value_list, axis=1)
    query_return, key_return, value_return = (
        lax.all_to_all(
            query_input.astype(jnp.bfloat16), "seq", split_axis=0, concat_axis=1, tiled=True
        ).astype(query_input.dtype),
        lax.all_to_all(
            key_input.astype(jnp.bfloat16), "seq", split_axis=0, concat_axis=1, tiled=True
        ).astype(key_input.dtype),
        lax.all_to_all(
            value_input.astype(jnp.bfloat16), "seq", split_axis=0, concat_axis=1, tiled=True
        ).astype(value_input.dtype),
    )
    grad_q = query_return.astype(jnp.bfloat16)
    grad_k = jnp.sum(key_return.reshape(local, kv_heads, group, width), axis=2).astype(jnp.bfloat16)
    grad_v = jnp.sum(value_return.reshape(local, kv_heads, group, width), axis=2).astype(
        jnp.bfloat16
    )
    gain_totals = lax.psum((query_gain_part, key_gain_part), ("dp", "seq"))
    return (grad_q[None], grad_k[None], grad_v[None], gain_totals[0], gain_totals[1])


def solution(mesh):
    return jax.shard_map(
        body,
        mesh=mesh,
        in_specs=(
            P("dp", "seq", None, None),
            P("dp", "seq", None, None),
            P("dp", "seq", None, None),
            P("dp", "seq", None, None),
            P("dp", "seq"),
            P(),
            P(),
        ),
        out_specs=(
            P("dp", "seq", None, None),
            P("dp", "seq", None, None),
            P("dp", "seq", None, None),
            P(),
            P(),
        ),
        check_vma=False,
    )
```

profile of v0, /device:TPU:1, one launch (start us, length us, event | category | flops | bytes accessed | tf_op | source)
XLA Modules:
  0.0 308.5 jit_solution(509402824562934716)
XLA Ops:
  2.6 7.7 %all-to-all-start = ((bf16[128,16,128]{2,0,1:T(8,128)(2,1)}), bf16[128,16,128]{2,0,1:T(8,128)(2,1)S(1)}, u32[]{:S(2)}, u32[]{:S(2)}) async-start(bf16[128,16,128]{2,0,1:T(8,128)(2,1)} %bitcast.130), calls=%async_computation | async-start | bytes 1048576 | tf_op jit(solution)/shard_map/all_to_all | solution.py:158
  10.4 17.6 %all_gather.3 = s32[1,2048]{1,0:T(1,128)S(1)} all-gather(s32[1,128]{1,0:T(1,128)S(1)} %copy-done.13), channel_id=1, replica_groups=mesh['dp'=32,'seq'=16] {'seq'}, dimensions={1}, use_global_device_ids=true | all-gather | bytes 8704 | tf_op jit(solution)/shard_map/all_gather | solution.py:144
  31.3 4.0 %all-to-all-start.1 = ((bf16[128,16,128]{0,2,1:T(8,128)(2,1)}), bf16[128,16,128]{0,2,1:T(8,128)(2,1)S(1)}, u32[]{:S(2)}, u32[]{:S(2)}) async-start(bf16[128,16,128]{0,2,1:T(8,128)(2,1)} %bitcast.12), calls=%async_computation.1 | async-start | bytes 1048576 | tf_op jit(solution)/shard_map/all_to_all | solution.py:160
  37.4 6.9 %all-to-all-done.1 = bf16[128,16,128]{0,2,1:T(8,128)(2,1)S(1)} async-done(((bf16[128,16,128]{0,2,1:T(8,128)(2,1)}), bf16[128,16,128]{0,2,1:T(8,128)(2,1)S(1)}, u32[]{:S(2)}, u32[]{:S(2)}) %all-to-all-start.1) | async-done | bytes 524320 | tf_op jit(solution)/shard_map/all_to_all | solution.py:160
  45.3 3.6 %all-to-all-start.2 = ((bf16[128,16,128]{2,0,1:T(8,128)(2,1)}), bf16[128,16,128]{2,0,1:T(8,128)(2,1)S(1)}, u32[]{:S(2)}, u32[]{:S(2)}) async-start(bf16[128,16,128]{2,0,1:T(8,128)(2,1)} %bitcast.20), calls=%async_computation.2 | async-start | bytes 1048576 | tf_op jit(solution)/shard_map/all_to_all | solution.py:161
  50.8 7.0 %all-to-all-done.2 = bf16[128,16,128]{2,0,1:T(8,128)(2,1)S(1)} async-done(((bf16[128,16,128]{2,0,1:T(8,128)(2,1)}), bf16[128,16,128]{2,0,1:T(8,128)(2,1)S(1)}, u32[]{:S(2)}, u32[]{:S(2)}) %all-to-all-start.2) | async-done | bytes 524320 | tf_op jit(solution)/shard_map/all_to_all | solution.py:161
  57.8 4.2 %all-to-all-start.3 = ((bf16[128,16,128]{2,0,1:T(8,128)(2,1)}), bf16[128,16,128]{2,0,1:T(8,128)(2,1)}, u32[]{:S(2)}, u32[]{:S(2)}) async-start(bf16[128,16,128]{2,0,1:T(8,128)(2,1)} %bitcast.129), calls=%async_computation.3 | async-start | bytes 1048576 | tf_op jit(solution)/shard_map/all_to_all | solution.py:159
  62.1 3.1 fusion.63
  66.2 4.8 %all-to-all-done.3 = bf16[128,16,128]{2,0,1:T(8,128)(2,1)} async-done(((bf16[128,16,128]{2,0,1:T(8,128)(2,1)}), bf16[128,16,128]{2,0,1:T(8,128)(2,1)}, u32[]{:S(2)}, u32[]{:S(2)}) %all-to-all-start.3) | async-done | bytes 524320 | tf_op jit(solution)/shard_map/all_to_all | solution.py:159
  72.3 69.1 %while.79 = (s32[]{:T(128)}, f32[2048,128]{0,1:T(8,128)}, f32[2048,128]{1,0:T(8,128)S(1)}, f32[2048,128]{1,0:T(8,128)S(1)}, bf16[2048,1,128]{0,2,1:T(8,128)(2,1)...) while((s32[]{:T(128)}, f32[2048,128]{0,1:T(8,128)}, ...), condition=%wide.region_12.13_spmd, body=%wide.region_5.12_spmd.sunk | while | flops 475268608 | bytes 14478353 | solution.py:139
  76.3 3.7 %while.81 = (s32[]{:T(128)}, f32[512,128]{1,0:T(8,128)S(1)}, f32[2048,128]{1,0:T(8,128)S(1)}, f32[2048,128]{1,0:T(8,128)S(1)}, s32[]{:T(128)}, /*index=5*/s32[51...) while((s32[]{:T(128)}, f32[512,128]{1,0:T(8,128)S(1)}, ...), condition=%wide.region_11.11_spmd.clone, body=%wide.region_10.10_spmd.clone.sunk | while | flops 338887680 | bytes 5656819 | solution.py:125
  82.1 3.7 %while.80 = (s32[]{:T(128)}, f32[512]{0:T(512)S(1)}, f32[512,128]{1,0:T(8,128)S(1)}, s32[]{:T(128)}, s32[512]{0:T(512)S(1)}, /*index=5*/s32[2048]{0:T(1024)S(1)}...) while((s32[]{:T(128)}, f32[512]{0:T(512)S(1)}, ...), condition=%wide.region_8.8_spmd.clone, body=%wide.region_6.7_spmd.clone.sunk | while | flops 136119296 | bytes 1990855 | solution.py:82
  87.0 7.4 %while.81 = (s32[]{:T(128)}, f32[512,128]{1,0:T(8,128)S(1)}, f32[2048,128]{1,0:T(8,128)S(1)}, f32[2048,128]{1,0:T(8,128)S(1)}, s32[]{:T(128)}, /*index=5*/s32[51...) while((s32[]{:T(128)}, f32[512,128]{1,0:T(8,128)S(1)}, ...), condition=%wide.region_11.11_spmd.clone, body=%wide.region_10.10_spmd.clone.sunk | while | flops 338887680 | bytes 5656819 | solution.py:125
  96.6 5.6 %while.80 = (s32[]{:T(128)}, f32[512]{0:T(512)S(1)}, f32[512,128]{1,0:T(8,128)S(1)}, s32[]{:T(128)}, s32[512]{0:T(512)S(1)}, /*index=5*/s32[2048]{0:T(1024)S(1)}...) while((s32[]{:T(128)}, f32[512]{0:T(512)S(1)}, ...), condition=%wide.region_8.8_spmd.clone, body=%wide.region_6.7_spmd.clone.sunk | while | flops 136119296 | bytes 1990855 | solution.py:82
  103.4 11.1 %while.81 = (s32[]{:T(128)}, f32[512,128]{1,0:T(8,128)S(1)}, f32[2048,128]{1,0:T(8,128)S(1)}, f32[2048,128]{1,0:T(8,128)S(1)}, s32[]{:T(128)}, /*index=5*/s32[51...) while((s32[]{:T(128)}, f32[512,128]{1,0:T(8,128)S(1)}, ...), condition=%wide.region_11.11_spmd.clone, body=%wide.region_10.10_spmd.clone.sunk | while | flops 338887680 | bytes 5656819 | solution.py:125
  116.6 7.5 %while.80 = (s32[]{:T(128)}, f32[512]{0:T(512)S(1)}, f32[512,128]{1,0:T(8,128)S(1)}, s32[]{:T(128)}, s32[512]{0:T(512)S(1)}, /*index=5*/s32[2048]{0:T(1024)S(1)}...) while((s32[]{:T(128)}, f32[512]{0:T(512)S(1)}, ...), condition=%wide.region_8.8_spmd.clone, body=%wide.region_6.7_spmd.clone.sunk | while | flops 136119296 | bytes 1990855 | solution.py:82
  125.3 14.8 %while.81 = (s32[]{:T(128)}, f32[512,128]{1,0:T(8,128)S(1)}, f32[2048,128]{1,0:T(8,128)S(1)}, f32[2048,128]{1,0:T(8,128)S(1)}, s32[]{:T(128)}, /*index=5*/s32[51...) while((s32[]{:T(128)}, f32[512,128]{1,0:T(8,128)S(1)}, ...), condition=%wide.region_11.11_spmd.clone, body=%wide.region_10.10_spmd.clone.sunk | while | flops 338887680 | bytes 5656819 | solution.py:125
  142.7 4.1 %fusion.60 = (f32[2048,1,64]{0,2,1:T(8,128)S(1)}, f32[2048,1,64]{0,2,1:T(8,128)S(1)}, f32[2048,1,64]{0,2,1:T(8,128)S(1)}, f32[2048,1,64]{0,2,1:T(8,128)S(1)}) fusion(f32[2048,1,128]{0,2,1:T(8,128)} %bitcast.158, f32[64]{0:T(128)S(1)} %negate_power_fusion, f32[2048]{0:T(1024)S(1)} %convert_multiply_fusion.1, f32[2048,1,128]{0,2,1:T(8,128)} %bitcast.157), kind=kLoop, calls=%fused_computation.89 | loop fusion | flops 1966080 | bytes 4202752 | tf_op jit(solution)/shard_map/transpose(jvp())/add_any | solution.py:34
  151.6 3.6 %all-to-all-start.4 = ((bf16[16,2,8192]{2,1,0:T(2,128)(2,1)}), bf16[16,2,8192]{2,1,0:T(2,128)(2,1)S(1)}, u32[]{:S(2)}, u32[]{:S(2)}) async-start(bf16[16,2,8192]{2,1,0:T(2,128)(2,1)} %reshape.576), calls=%async_computation.4 | async-start | bytes 1048576 | tf_op jit(solution)/shard_map/all_to_all | solution.py:178
  157.4 6.8 %all-to-all-done.4 = bf16[16,2,8192]{2,1,0:T(2,128)(2,1)S(1)} async-done(((bf16[16,2,8192]{2,1,0:T(2,128)(2,1)}), bf16[16,2,8192]{2,1,0:T(2,128)(2,1)S(1)}, u32[]{:S(2)}, u32[]{:S(2)}) %all-to-all-start.4) | async-done | bytes 524320 | tf_op jit(solution)/shard_map/all_to_all | solution.py:178
  164.1 3.6 %all-to-all-start.5 = ((bf16[16,2,8192]{2,1,0:T(2,128)(2,1)}), bf16[16,2,8192]{2,1,0:T(2,128)(2,1)S(1)}, u32[]{:S(2)}, u32[]{:S(2)}) async-start(bf16[16,2,8192]{2,1,0:T(2,128)(2,1)} %reshape.578), calls=%async_computation.5 | async-start | bytes 1048576 | tf_op jit(solution)/shard_map/all_to_all | solution.py:181
  169.7 9.0 %all-to-all-done.5 = bf16[16,2,8192]{2,1,0:T(2,128)(2,1)S(1)} async-done(((bf16[16,2,8192]{2,1,0:T(2,128)(2,1)}), bf16[16,2,8192]{2,1,0:T(2,128)(2,1)S(1)}, u32[]{:S(2)}, u32[]{:S(2)}) %all-to-all-start.5) | async-done | bytes 524320 | tf_op jit(solution)/shard_map/all_to_all | solution.py:181
  178.7 3.6 %all-to-all-start.6 = ((bf16[16,2,8192]{2,1,0:T(2,128)(2,1)}), bf16[16,2,8192]{2,1,0:T(2,128)(2,1)S(1)}, u32[]{:S(2)}, u32[]{:S(2)}) async-start(bf16[16,2,8192]{2,1,0:T(2,128)(2,1)} %reshape.580), calls=%async_computation.6 | async-start | bytes 1048576 | tf_op jit(solution)/shard_map/all_to_all | solution.py:184
  182.3 121.2 %all-reduce.4 = (f32[128]{0:T(128)}, f32[128]{0:T(128)}) all-reduce(f32[128]{0:T(128)S(1)} %get-tuple-element.430, f32[128]{0:T(128)S(1)} %get-tuple-element.428), channel_id=1, replica_groups=mesh['dp'=32,'seq'=16] {'dp','seq'}, use_global_device_ids=true, to_apply=%region_18.19 | all-reduce | flops 256 | bytes 2048 | tf_op jit(solution)/shard_map/psum | solution.py:193
  (256 shorter events, 97.5 us)
Async XLA Ops:
  2.6 7.7 %copy-start.13 = (s32[1,128]{1,0:T(1,128)S(1)}, s32[1,128]{1,0:T(1,128)}, u32[]{:S(2)}) copy-start(s32[1,128]{1,0:T(1,128)} %param.17) | copy-start | bytes 1540
  2.6 25.7 %copy-start.9 = (bf16[1,128,8,128]{3,2,1,0:T(8,128)(2,1)S(1)}, bf16[1,128,8,128]{3,2,1,0:T(8,128)(2,1)}, u32[]{:S(2)}) copy-start(bf16[1,128,8,128]{3,2,1,0:T(8,128)(2,1)} %param.14) | copy-start | bytes 786436
  2.6 27.8 %all-to-all-start = ((bf16[128,16,128]{2,0,1:T(8,128)(2,1)}), bf16[128,16,128]{2,0,1:T(8,128)(2,1)S(1)}, u32[]{:S(2)}, u32[]{:S(2)}) async-start(bf16[128,16,128]{2,0,1:T(8,128)(2,1)} %bitcast.130), calls=%async_computation | async-start | bytes 1048576 | tf_op jit(solution)/shard_map/all_to_all | solution.py:158
  10.3 18.2 %copy-start.10 = (bf16[1,128,8,128]{3,2,1,0:T(8,128)(2,1)S(1)}, bf16[1,128,8,128]{3,2,1,0:T(8,128)(2,1)}, u32[]{:S(2)}) copy-start(bf16[1,128,8,128]{3,2,1,0:T(8,128)(2,1)} %param.15) | copy-start | bytes 786436
  28.3 1.0 copy-start.8
  31.3 13.0 %all-to-all-start.1 = ((bf16[128,16,128]{0,2,1:T(8,128)(2,1)}), bf16[128,16,128]{0,2,1:T(8,128)(2,1)S(1)}, u32[]{:S(2)}, u32[]{:S(2)}) async-start(bf16[128,16,128]{0,2,1:T(8,128)(2,1)} %bitcast.12), calls=%async_computation.1 | async-start | bytes 1048576 | tf_op jit(solution)/shard_map/all_to_all | solution.py:160
  36.5 1.0 copy-start
  44.3 4.7 %copy-start.2 = (bf16[128,16,128]{0,2,1:T(8,128)(2,1)}, bf16[128,16,128]{0,2,1:T(8,128)(2,1)S(1)}, u32[]{:S(2)}) copy-start(bf16[128,16,128]{0,2,1:T(8,128)(2,1)S(1)} %all-to-all-done.1) | copy-start | bytes 1572868
  45.3 12.5 %all-to-all-start.2 = ((bf16[128,16,128]{2,0,1:T(8,128)(2,1)}), bf16[128,16,128]{2,0,1:T(8,128)(2,1)S(1)}, u32[]{:S(2)}, u32[]{:S(2)}) async-start(bf16[128,16,128]{2,0,1:T(8,128)(2,1)} %bitcast.20), calls=%async_computation.2 | async-start | bytes 1048576 | tf_op jit(solution)/shard_map/all_to_all | solution.py:161
  50.8 11.2 %copy-start.4 = (f32[2048,1,128]{0,2,1:T(8,128)S(1)}, f32[2048,1,128]{0,2,1:T(8,128)}, u32[]{:S(2)}) copy-start(f32[2048,1,128]{0,2,1:T(8,128)} %fusion.33) | copy-start | bytes 3145732
  57.8 13.2 %all-to-all-start.3 = ((bf16[128,16,128]{2,0,1:T(8,128)(2,1)}), bf16[128,16,128]{2,0,1:T(8,128)(2,1)}, u32[]{:S(2)}, u32[]{:S(2)}) async-start(bf16[128,16,128]{2,0,1:T(8,128)(2,1)} %bitcast.129), calls=%async_computation.3 | async-start | bytes 1048576 | tf_op jit(solution)/shard_map/all_to_all | solution.py:159
  65.2 1.0 copy-start.7
  72.4 0.8 copy-start.5
  80.1 1.1 copy-start.6
  94.6 1.1 copy-start.6
  95.7 0.8 copy-start.5
  114.6 1.1 copy-start.6
  115.8 0.8 copy-start.5
  140.3 1.1 copy-start.6
  142.7 4.1 %copy-start.3 = (bf16[128,16,128]{0,2,1:T(8,128)(2,1)S(1)}, bf16[128,16,128]{0,2,1:T(8,128)(2,1)}, u32[]{:S(2)}) copy-start(bf16[128,16,128]{0,2,1:T(8,128)(2,1)} %copy-done.2) | copy-start | bytes 1572868
  146.8 1.2 copy-start.1
  151.6 12.5 %all-to-all-start.4 = ((bf16[16,2,8192]{2,1,0:T(2,128)(2,1)}), bf16[16,2,8192]{2,1,0:T(2,128)(2,1)S(1)}, u32[]{:S(2)}, u32[]{:S(2)}) async-start(bf16[16,2,8192]{2,1,0:T(2,128)(2,1)} %reshape.576), calls=%async_computation.4 | async-start | bytes 1048576 | tf_op jit(solution)/shard_map/all_to_all | solution.py:178
  164.1 14.6 %all-to-all-start.5 = ((bf16[16,2,8192]{2,1,0:T(2,128)(2,1)}), bf16[16,2,8192]{2,1,0:T(2,128)(2,1)S(1)}, u32[]{:S(2)}, u32[]{:S(2)}) async-start(bf16[16,2,8192]{2,1,0:T(2,128)(2,1)} %reshape.578), calls=%async_computation.5 | async-start | bytes 1048576 | tf_op jit(solution)/shard_map/all_to_all | solution.py:181
  178.7 128.1 %all-to-all-start.6 = ((bf16[16,2,8192]{2,1,0:T(2,128)(2,1)}), bf16[16,2,8192]{2,1,0:T(2,128)(2,1)S(1)}, u32[]{:S(2)}, u32[]{:S(2)}) async-start(bf16[16,2,8192]{2,1,0:T(2,128)(2,1)} %reshape.580), calls=%async_computation.6 | async-start | bytes 1048576 | tf_op jit(solution)/shard_map/all_to_all | solution.py:184
  (3 other events, 2.1 us)
where the time goes:
time: 310 us; the launch traced here: 308 us
  blocking collectives  139 us (45%)
  matrix products  53.1 us (17%)
  waiting for transfers between devices  34.4 us (11%)
  local copies, waits for them, and re-layouts  30.6 us (10%)
  starting transfers between devices  30.2 us (10%)
  other arithmetic  19 us (6%)
    psum x1, blocking collectives, body(): gain_totals = lax.psum((query_gain_part, key_gain_part), ('dp', 'seq'))  121 us
    dot_general x20, matrix products, key_scores(): lax.dot_general(query_rows, key_rows, contract_last, preferred_element_ty...  27.3 us
    all_gather x1, blocking collectives, body(): segments = lax.all_gather(segment_ids, 'seq', axis=1, tiled=True)[0]  17.6 us
    unnamed x40, local copies, waits for them, and re-layouts  14.1 us
    dot_general x10, matrix products, backward_step(): jnp.dot(score_grads, key_rows, preferred_element_type=jnp.float32)  12.8 us
    all_to_all x1, waiting for transfers between devices, body(): lax.all_to_all(key_input.astype(jnp.bfloat16), 'seq', split_axis=0, conca...  8.96 us
    all_to_all x1, starting transfers between devices, body(): lax.all_to_all(q_pre[0], 'seq', split_axis=1, concat_axis=0, tiled=True)  7.72 us
    all_to_all x1, waiting for transfers between devices, body(): lax.all_to_all(value_copies, 'seq', split_axis=1, concat_axis=0, tiled=True)  6.98 us
  transfers between devices with their start and end apart: 7, of which 5 were waited for; matrix products, arithmetic and copies ran while one was open for 5% of the time, Pallas kernels for 0%

commit v1 on v0

--- a/solution.py
+++ b/solution.py
@@ -190,7 +190,7 @@
     grad_v = jnp.sum(value_return.reshape(local, kv_heads, group, width), axis=2).astype(
         jnp.bfloat16
     )
-    gain_totals = lax.psum((query_gain_part, key_gain_part), ("dp", "seq"))
+    gain_totals = lax.psum(lax.psum((query_gain_part, key_gain_part), "seq"), "dp")
     return (grad_q[None], grad_k[None], grad_v[None], gain_totals[0], gain_totals[1])
 
 

time: 310 us -> 295 us (0.952)
  blocking collectives: 139 us -> 124 us
    psum x1 -> x2, blocking collectives: 121 us -> 106 us  [the longest x1 72 us: body(): lax.psum(lax.psum((query_gain_part, key_gain_part), 'seq'), 'dp')]
where the time goes in v1:
time: 295 us; the launch traced here: 293 us
  blocking collectives  124 us (42%)
  matrix products  53.1 us (18%)
  waiting for transfers between devices  34.4 us (12%)
  local copies, waits for them, and re-layouts  30.6 us (10%)
  starting transfers between devices  30.2 us (10%)
  other arithmetic  19 us (6%)
    psum x1, blocking collectives, body(): lax.psum(lax.psum((query_gain_part, key_gain_part), 'seq'), 'dp')  72 us
    psum x1, blocking collectives, body(): lax.psum((query_gain_part, key_gain_part), 'seq')  34.3 us
    dot_general x20, matrix products, key_scores(): lax.dot_general(query_rows, key_rows, contract_last, preferred_element_ty...  27.3 us
    all_gather x1, blocking collectives, body(): segments = lax.all_gather(segment_ids, 'seq', axis=1, tiled=True)[0]  17.6 us
    unnamed x40, local copies, waits for them, and re-layouts  14.1 us
    dot_general x10, matrix products, backward_step(): jnp.dot(score_grads, key_rows, preferred_element_type=jnp.float32)  12.8 us
    all_to_all x1, waiting for transfers between devices, body(): lax.all_to_all(key_input.astype(jnp.bfloat16), 'seq', split_axis=0, conca...  8.96 us
    all_to_all x1, starting transfers between devices, body(): lax.all_to_all(q_pre[0], 'seq', split_axis=1, concat_axis=0, tiled=True)  7.72 us
  transfers between devices with their start and end apart: 7, of which 5 were waited for; matrix products, arithmetic and copies ran while one was open for 5% of the time, Pallas kernels for 0%

profile of v1, /device:TPU:1, one launch (start us, length us, event | category | flops | bytes accessed | tf_op | source)
XLA Modules:
  0.0 293.5 jit_solution(402039611458420183)
XLA Ops:
  2.6 7.7 %all-to-all-start = ((bf16[128,16,128]{2,0,1:T(8,128)(2,1)}), bf16[128,16,128]{2,0,1:T(8,128)(2,1)S(1)}, u32[]{:S(2)}, u32[]{:S(2)}) async-start(bf16[128,16,128]{2,0,1:T(8,128)(2,1)} %bitcast.130), calls=%async_computation | async-start | bytes 1048576 | tf_op jit(solution)/shard_map/all_to_all | solution.py:158
  10.4 17.6 %all_gather.3 = s32[1,2048]{1,0:T(1,128)S(1)} all-gather(s32[1,128]{1,0:T(1,128)S(1)} %copy-done.13), channel_id=1, replica_groups=mesh['dp'=32,'seq'=16] {'seq'}, dimensions={1}, use_global_device_ids=true | all-gather | bytes 8704 | tf_op jit(solution)/shard_map/all_gather | solution.py:144
  31.3 4.0 %all-to-all-start.1 = ((bf16[128,16,128]{0,2,1:T(8,128)(2,1)}), bf16[128,16,128]{0,2,1:T(8,128)(2,1)S(1)}, u32[]{:S(2)}, u32[]{:S(2)}) async-start(bf16[128,16,128]{0,2,1:T(8,128)(2,1)} %bitcast.12), calls=%async_computation.1 | async-start | bytes 1048576 | tf_op jit(solution)/shard_map/all_to_all | solution.py:160
  37.4 6.9 %all-to-all-done.1 = bf16[128,16,128]{0,2,1:T(8,128)(2,1)S(1)} async-done(((bf16[128,16,128]{0,2,1:T(8,128)(2,1)}), bf16[128,16,128]{0,2,1:T(8,128)(2,1)S(1)}, u32[]{:S(2)}, u32[]{:S(2)}) %all-to-all-start.1) | async-done | bytes 524320 | tf_op jit(solution)/shard_map/all_to_all | solution.py:160
  45.3 3.6 %all-to-all-start.2 = ((bf16[128,16,128]{2,0,1:T(8,128)(2,1)}), bf16[128,16,128]{2,0,1:T(8,128)(2,1)S(1)}, u32[]{:S(2)}, u32[]{:S(2)}) async-start(bf16[128,16,128]{2,0,1:T(8,128)(2,1)} %bitcast.20), calls=%async_computation.2 | async-start | bytes 1048576 | tf_op jit(solution)/shard_map/all_to_all | solution.py:161
  50.8 7.0 %all-to-all-done.2 = bf16[128,16,128]{2,0,1:T(8,128)(2,1)S(1)} async-done(((bf16[128,16,128]{2,0,1:T(8,128)(2,1)}), bf16[128,16,128]{2,0,1:T(8,128)(2,1)S(1)}, u32[]{:S(2)}, u32[]{:S(2)}) %all-to-all-start.2) | async-done | bytes 524320 | tf_op jit(solution)/shard_map/all_to_all | solution.py:161
  57.8 4.2 %all-to-all-start.3 = ((bf16[128,16,128]{2,0,1:T(8,128)(2,1)}), bf16[128,16,128]{2,0,1:T(8,128)(2,1)}, u32[]{:S(2)}, u32[]{:S(2)}) async-start(bf16[128,16,128]{2,0,1:T(8,128)(2,1)} %bitcast.129), calls=%async_computation.3 | async-start | bytes 1048576 | tf_op jit(solution)/shard_map/all_to_all | solution.py:159
  66.2 4.8 %all-to-all-done.3 = bf16[128,16,128]{2,0,1:T(8,128)(2,1)} async-done(((bf16[128,16,128]{2,0,1:T(8,128)(2,1)}), bf16[128,16,128]{2,0,1:T(8,128)(2,1)}, u32[]{:S(2)}, u32[]{:S(2)}) %all-to-all-start.3) | async-done | bytes 524320 | tf_op jit(solution)/shard_map/all_to_all | solution.py:159
  72.3 69.1 %while.79 = (s32[]{:T(128)}, f32[2048,128]{0,1:T(8,128)}, f32[2048,128]{1,0:T(8,128)S(1)}, f32[2048,128]{1,0:T(8,128)S(1)}, bf16[2048,1,128]{0,2,1:T(8,128)(2,1)...) while((s32[]{:T(128)}, f32[2048,128]{0,1:T(8,128)}, ...), condition=%wide.region_12.13_spmd, body=%wide.region_5.12_spmd.sunk | while | flops 475268608 | bytes 14478353 | solution.py:139
  76.3 3.7 %while.81 = (s32[]{:T(128)}, f32[512,128]{1,0:T(8,128)S(1)}, f32[2048,128]{1,0:T(8,128)S(1)}, f32[2048,128]{1,0:T(8,128)S(1)}, s32[]{:T(128)}, /*index=5*/s32[51...) while((s32[]{:T(128)}, f32[512,128]{1,0:T(8,128)S(1)}, ...), condition=%wide.region_11.11_spmd.clone, body=%wide.region_10.10_spmd.clone.sunk | while | flops 338887680 | bytes 5656819 | solution.py:125
  82.1 3.7 %while.80 = (s32[]{:T(128)}, f32[512]{0:T(512)S(1)}, f32[512,128]{1,0:T(8,128)S(1)}, s32[]{:T(128)}, s32[512]{0:T(512)S(1)}, /*index=5*/s32[2048]{0:T(1024)S(1)}...) while((s32[]{:T(128)}, f32[512]{0:T(512)S(1)}, ...), condition=%wide.region_8.8_spmd.clone, body=%wide.region_6.7_spmd.clone.sunk | while | flops 136119296 | bytes 1990855 | solution.py:82
  87.0 7.4 %while.81 = (s32[]{:T(128)}, f32[512,128]{1,0:T(8,128)S(1)}, f32[2048,128]{1,0:T(8,128)S(1)}, f32[2048,128]{1,0:T(8,128)S(1)}, s32[]{:T(128)}, /*index=5*/s32[51...) while((s32[]{:T(128)}, f32[512,128]{1,0:T(8,128)S(1)}, ...), condition=%wide.region_11.11_spmd.clone, body=%wide.region_10.10_spmd.clone.sunk | while | flops 338887680 | bytes 5656819 | solution.py:125
  96.6 5.6 %while.80 = (s32[]{:T(128)}, f32[512]{0:T(512)S(1)}, f32[512,128]{1,0:T(8,128)S(1)}, s32[]{:T(128)}, s32[512]{0:T(512)S(1)}, /*index=5*/s32[2048]{0:T(1024)S(1)}...) while((s32[]{:T(128)}, f32[512]{0:T(512)S(1)}, ...), condition=%wide.region_8.8_spmd.clone, body=%wide.region_6.7_spmd.clone.sunk | while | flops 136119296 | bytes 1990855 | solution.py:82
  103.4 11.1 %while.81 = (s32[]{:T(128)}, f32[512,128]{1,0:T(8,128)S(1)}, f32[2048,128]{1,0:T(8,128)S(1)}, f32[2048,128]{1,0:T(8,128)S(1)}, s32[]{:T(128)}, /*index=5*/s32[51...) while((s32[]{:T(128)}, f32[512,128]{1,0:T(8,128)S(1)}, ...), condition=%wide.region_11.11_spmd.clone, body=%wide.region_10.10_spmd.clone.sunk | while | flops 338887680 | bytes 5656819 | solution.py:125
  116.6 7.5 %while.80 = (s32[]{:T(128)}, f32[512]{0:T(512)S(1)}, f32[512,128]{1,0:T(8,128)S(1)}, s32[]{:T(128)}, s32[512]{0:T(512)S(1)}, /*index=5*/s32[2048]{0:T(1024)S(1)}...) while((s32[]{:T(128)}, f32[512]{0:T(512)S(1)}, ...), condition=%wide.region_8.8_spmd.clone, body=%wide.region_6.7_spmd.clone.sunk | while | flops 136119296 | bytes 1990855 | solution.py:82
  125.3 14.8 %while.81 = (s32[]{:T(128)}, f32[512,128]{1,0:T(8,128)S(1)}, f32[2048,128]{1,0:T(8,128)S(1)}, f32[2048,128]{1,0:T(8,128)S(1)}, s32[]{:T(128)}, /*index=5*/s32[51...) while((s32[]{:T(128)}, f32[512,128]{1,0:T(8,128)S(1)}, ...), condition=%wide.region_11.11_spmd.clone, body=%wide.region_10.10_spmd.clone.sunk | while | flops 338887680 | bytes 5656819 | solution.py:125
  142.7 4.1 %fusion.60 = (f32[2048,1,64]{0,2,1:T(8,128)S(1)}, f32[2048,1,64]{0,2,1:T(8,128)S(1)}, f32[2048,1,64]{0,2,1:T(8,128)S(1)}, f32[2048,1,64]{0,2,1:T(8,128)S(1)}) fusion(f32[2048,1,128]{0,2,1:T(8,128)} %bitcast.158, f32[64]{0:T(128)S(1)} %negate_power_fusion, f32[2048]{0:T(1024)S(1)} %convert_multiply_fusion.1, f32[2048,1,128]{0,2,1:T(8,128)} %bitcast.157), kind=kLoop, calls=%fused_computation.89 | loop fusion | flops 1966080 | bytes 4202752 | tf_op jit(solution)/shard_map/transpose(jvp())/add_any | solution.py:34
  151.6 3.6 %all-to-all-start.4 = ((bf16[16,2,8192]{2,1,0:T(2,128)(2,1)}), bf16[16,2,8192]{2,1,0:T(2,128)(2,1)S(1)}, u32[]{:S(2)}, u32[]{:S(2)}) async-start(bf16[16,2,8192]{2,1,0:T(2,128)(2,1)} %reshape.576), calls=%async_computation.4 | async-start | bytes 1048576 | tf_op jit(solution)/shard_map/all_to_all | solution.py:178
  157.4 6.8 %all-to-all-done.4 = bf16[16,2,8192]{2,1,0:T(2,128)(2,1)S(1)} async-done(((bf16[16,2,8192]{2,1,0:T(2,128)(2,1)}), bf16[16,2,8192]{2,1,0:T(2,128)(2,1)S(1)}, u32[]{:S(2)}, u32[]{:S(2)}) %all-to-all-start.4) | async-done | bytes 524320 | tf_op jit(solution)/shard_map/all_to_all | solution.py:178
  164.1 3.6 %all-to-all-start.5 = ((bf16[16,2,8192]{2,1,0:T(2,128)(2,1)}), bf16[16,2,8192]{2,1,0:T(2,128)(2,1)S(1)}, u32[]{:S(2)}, u32[]{:S(2)}) async-start(bf16[16,2,8192]{2,1,0:T(2,128)(2,1)} %reshape.578), calls=%async_computation.5 | async-start | bytes 1048576 | tf_op jit(solution)/shard_map/all_to_all | solution.py:181
  169.7 9.0 %all-to-all-done.5 = bf16[16,2,8192]{2,1,0:T(2,128)(2,1)S(1)} async-done(((bf16[16,2,8192]{2,1,0:T(2,128)(2,1)}), bf16[16,2,8192]{2,1,0:T(2,128)(2,1)S(1)}, u32[]{:S(2)}, u32[]{:S(2)}) %all-to-all-start.5) | async-done | bytes 524320 | tf_op jit(solution)/shard_map/all_to_all | solution.py:181
  178.7 3.6 %all-to-all-start.6 = ((bf16[16,2,8192]{2,1,0:T(2,128)(2,1)}), bf16[16,2,8192]{2,1,0:T(2,128)(2,1)S(1)}, u32[]{:S(2)}, u32[]{:S(2)}) async-start(bf16[16,2,8192]{2,1,0:T(2,128)(2,1)} %reshape.580), calls=%async_computation.6 | async-start | bytes 1048576 | tf_op jit(solution)/shard_map/all_to_all | solution.py:184
  182.3 34.3 %all-reduce.5 = (f32[128]{0:T(128)S(1)}, f32[128]{0:T(128)S(1)}) all-reduce(f32[128]{0:T(128)S(1)} %get-tuple-element.430, f32[128]{0:T(128)S(1)} %get-tuple-element.428), channel_id=1, replica_groups=mesh['dp'=32,'seq'=16] {'seq'}, use_global_device_ids=true, to_apply=%region_18.19 | all-reduce | flops 256 | bytes 2048 | tf_op jit(solution)/shard_map/psum | solution.py:193
  216.5 72.0 %all-reduce.4 = (f32[128]{0:T(128)}, f32[128]{0:T(128)}) all-reduce(f32[128]{0:T(128)S(1)} %get-tuple-element.500, f32[128]{0:T(128)S(1)} %get-tuple-element.501), channel_id=1, replica_groups=mesh['dp'=32,'seq'=16] {'dp'}, use_global_device_ids=true, to_apply=%region_19.20 | all-reduce | flops 256 | bytes 2048 | tf_op jit(solution)/shard_map/psum | solution.py:193
  (257 shorter events, 100.5 us)
Async XLA Ops:
  2.6 7.7 %copy-start.13 = (s32[1,128]{1,0:T(1,128)S(1)}, s32[1,128]{1,0:T(1,128)}, u32[]{:S(2)}) copy-start(s32[1,128]{1,0:T(1,128)} %param.17) | copy-start | bytes 1540
  2.6 25.7 %copy-start.9 = (bf16[1,128,8,128]{3,2,1,0:T(8,128)(2,1)S(1)}, bf16[1,128,8,128]{3,2,1,0:T(8,128)(2,1)}, u32[]{:S(2)}) copy-start(bf16[1,128,8,128]{3,2,1,0:T(8,128)(2,1)} %param.14) | copy-start | bytes 786436
  2.6 27.8 %all-to-all-start = ((bf16[128,16,128]{2,0,1:T(8,128)(2,1)}), bf16[128,16,128]{2,0,1:T(8,128)(2,1)S(1)}, u32[]{:S(2)}, u32[]{:S(2)}) async-start(bf16[128,16,128]{2,0,1:T(8,128)(2,1)} %bitcast.130), calls=%async_computation | async-start | bytes 1048576 | tf_op jit(solution)/shard_map/all_to_all | solution.py:158
  10.3 18.2 %copy-start.10 = (bf16[1,128,8,128]{3,2,1,0:T(8,128)(2,1)S(1)}, bf16[1,128,8,128]{3,2,1,0:T(8,128)(2,1)}, u32[]{:S(2)}) copy-start(bf16[1,128,8,128]{3,2,1,0:T(8,128)(2,1)} %param.15) | copy-start | bytes 786436
  28.3 1.0 copy-start.8
  31.3 13.0 %all-to-all-start.1 = ((bf16[128,16,128]{0,2,1:T(8,128)(2,1)}), bf16[128,16,128]{0,2,1:T(8,128)(2,1)S(1)}, u32[]{:S(2)}, u32[]{:S(2)}) async-start(bf16[128,16,128]{0,2,1:T(8,128)(2,1)} %bitcast.12), calls=%async_computation.1 | async-start | bytes 1048576 | tf_op jit(solution)/shard_map/all_to_all | solution.py:160
  36.5 1.0 copy-start
  44.3 4.7 %copy-start.2 = (bf16[128,16,128]{0,2,1:T(8,128)(2,1)}, bf16[128,16,128]{0,2,1:T(8,128)(2,1)S(1)}, u32[]{:S(2)}) copy-start(bf16[128,16,128]{0,2,1:T(8,128)(2,1)S(1)} %all-to-all-done.1) | copy-start | bytes 1572868
  45.3 12.5 %all-to-all-start.2 = ((bf16[128,16,128]{2,0,1:T(8,128)(2,1)}), bf16[128,16,128]{2,0,1:T(8,128)(2,1)S(1)}, u32[]{:S(2)}, u32[]{:S(2)}) async-start(bf16[128,16,128]{2,0,1:T(8,128)(2,1)} %bitcast.20), calls=%async_computation.2 | async-start | bytes 1048576 | tf_op jit(solution)/shard_map/all_to_all | solution.py:161
  50.8 11.2 %copy-start.4 = (f32[2048,1,128]{0,2,1:T(8,128)S(1)}, f32[2048,1,128]{0,2,1:T(8,128)}, u32[]{:S(2)}) copy-start(f32[2048,1,128]{0,2,1:T(8,128)} %fusion.33) | copy-start | bytes 3145732
  57.8 13.2 %all-to-all-start.3 = ((bf16[128,16,128]{2,0,1:T(8,128)(2,1)}), bf16[128,16,128]{2,0,1:T(8,128)(2,1)}, u32[]{:S(2)}, u32[]{:S(2)}) async-start(bf16[128,16,128]{2,0,1:T(8,128)(2,1)} %bitcast.129), calls=%async_computation.3 | async-start | bytes 1048576 | tf_op jit(solution)/shard_map/all_to_all | solution.py:159
  65.2 1.0 copy-start.7
  72.4 0.8 copy-start.5
  80.1 1.1 copy-start.6
  94.6 1.1 copy-start.6
  95.7 0.8 copy-start.5
  114.6 1.1 copy-start.6
  115.8 0.8 copy-start.5
  140.3 1.1 copy-start.6
  142.7 4.1 %copy-start.3 = (bf16[128,16,128]{0,2,1:T(8,128)(2,1)S(1)}, bf16[128,16,128]{0,2,1:T(8,128)(2,1)}, u32[]{:S(2)}) copy-start(bf16[128,16,128]{0,2,1:T(8,128)(2,1)} %copy-done.2) | copy-start | bytes 1572868
  146.8 1.2 copy-start.1
  151.6 12.5 %all-to-all-start.4 = ((bf16[16,2,8192]{2,1,0:T(2,128)(2,1)}), bf16[16,2,8192]{2,1,0:T(2,128)(2,1)S(1)}, u32[]{:S(2)}, u32[]{:S(2)}) async-start(bf16[16,2,8192]{2,1,0:T(2,128)(2,1)} %reshape.576), calls=%async_computation.4 | async-start | bytes 1048576 | tf_op jit(solution)/shard_map/all_to_all | solution.py:178
  164.1 14.6 %all-to-all-start.5 = ((bf16[16,2,8192]{2,1,0:T(2,128)(2,1)}), bf16[16,2,8192]{2,1,0:T(2,128)(2,1)S(1)}, u32[]{:S(2)}, u32[]{:S(2)}) async-start(bf16[16,2,8192]{2,1,0:T(2,128)(2,1)} %reshape.578), calls=%async_computation.5 | async-start | bytes 1048576 | tf_op jit(solution)/shard_map/all_to_all | solution.py:181
  178.7 113.2 %all-to-all-start.6 = ((bf16[16,2,8192]{2,1,0:T(2,128)(2,1)}), bf16[16,2,8192]{2,1,0:T(2,128)(2,1)S(1)}, u32[]{:S(2)}, u32[]{:S(2)}) async-start(bf16[16,2,8192]{2,1,0:T(2,128)(2,1)} %reshape.580), calls=%async_computation.6 | async-start | bytes 1048576 | tf_op jit(solution)/shard_map/all_to_all | solution.py:184
  (3 other events, 2.1 us)
